TPU v7x, 32 devices: a whole 2x2x4 slice. The times are simulated.
32 devices in a mesh: dev: 16 (over z, y, core), rhs: 2 (over x).
Axes of the slice: x: 2, y: 2, z: 4, core: 2. Of those that a mesh axis runs over, the one named last changes fastest.
Arguments:
- top_adj: float32 [16, 32, 16, 256], P('rhs', 'dev'), may hold values from -6 to 6
- level1_adj: float32 [16, 16, 64, 128], P('rhs', 'dev'), may hold values from -6 to 6
- image_offsets: int32 [64, 2], P('rhs'), may hold values from -6 to 6
- image_weights: float32 [64], P('rhs'), may hold values from 0.2 to 1
- incidence: float32 [16, 2], replicated, may hold values from -0.6 to 0.6
- child_list: int32 [16, 4], replicated, may hold values from 0 to 63, as said below
- theta_index_top: int32 [128, 3], replicated, may hold values from 0 to 63
- theta_weight_top: float32 [128, 3], replicated, may hold values from -2.7 to 2.7
- phi_weight_top: float32 [32, 3], replicated, may hold values from -2.7 to 2.7
- theta_index_mid: int32 [64, 3], replicated, may hold values from 0 to 31
- theta_weight_mid: float32 [64, 3], replicated, may hold values from -2.7 to 2.7
- phi_weight_mid: float32 [16, 3], replicated, may hold values from -2.7 to 2.7
Outputs:
- level0_adj: float32 [16, 256, 512], P('rhs', 'dev')
Inputs may be any that keep to these rules, and one draw needn't show every extreme that they name: `child_list`: row b holds the middle-level boxes 4 b to 4 b + 3, each once.
All inputs are finite; a program needn't handle non-finite values.
Results may differ from a plain program's by a relative error of at most 0.0003.
Values sent between devices are 32-bit elements; how exact they have to be, the bound alone decides.
No kernel may reach another device: no remote copies, remote signals or barrier semaphores. Data moves between devices by JAX's collectives and lax.ppermute only.
A program may use at most 128 MiB of HBM per device.

v0:
```python
import math
import jax
import jax.numpy as jnp
from jax import lax
from jax.sharding import PartitionSpec as P

PHASE_TOP = 18.85
PHASE_MID = 9.42
LATTICE = 12.57


def padded_2(cells, sides, width):
    for axis, dim in sides:
        count = lax.axis_size(axis)
        head = lax.slice_in_dim(cells, 0, width, axis=dim)
        tail = lax.slice_in_dim(cells, cells.shape[dim] - width, cells.shape[dim], axis=dim)
        cells = jnp.concatenate(
            [
                lax.ppermute(tail, axis, [(i, (i + 1) % count) for i in range(count)]),
                cells,
                lax.ppermute(head, axis, [((i + 1) % count, i) for i in range(count)]),
            ],
            axis=dim,
        )
    return cells


def directions(theta_count, phi_ids, phi_count):
    theta = math.pi / theta_count * (jnp.arange(theta_count, dtype=jnp.float32) + 0.5)
    azimuth = 2.0 * math.pi / phi_count * phi_ids.astype(jnp.float32)
    sin_theta = jnp.sin(theta)
    along_x = jnp.cos(azimuth)[:, None] * sin_theta[None, :]
    along_y = jnp.sin(azimuth)[:, None] * sin_theta[None, :]
    along_z = jnp.cos(theta)
    return (along_x, along_y, along_z)


def theta_matrix(index, weight, columns):
    hits = (index[:, :, None] == jnp.arange(columns, dtype=jnp.int32)[None, None, :]).astype(
        jnp.float32
    )
    return jnp.sum(weight[:, :, None] * hits, axis=1)


def phi_matrix(weight, row_ids, coarse_count, column_ids):
    target = (row_ids[:, None] // 2 + jnp.arange(3, dtype=jnp.int32)[None, :] - 1) % coarse_count
    hits = (target[:, :, None] == column_ids[None, None, :]).astype(jnp.float32)
    return jnp.sum(weight[:, :, None] * hits, axis=1)


def octant_phase(factor, octant, along_x, along_y, along_z):
    sign_x = 2.0 * (octant % 2) - 1.0
    sign_y = 2.0 * (octant // 2) - 1.0
    angle = factor * (sign_x * along_x + sign_y * along_y - along_z[None, :])
    return (jnp.cos(angle), jnp.sin(angle))


def lattice_sum(offsets, weighted, incident, along_x, along_y):
    phase_arg = LATTICE * (
        offsets[:, 0, None, None, None] * (along_x[None, None] - incident[None, :, 0, None, None])
        + offsets[:, 1, None, None, None] * (along_y[None, None] - incident[None, :, 1, None, None])
    )
    sum_real = jnp.sum(weighted[:, None, None, None] * jnp.cos(phase_arg), axis=0)
    sum_imag = jnp.sum(weighted[:, None, None, None] * jnp.sin(phase_arg), axis=0)
    return (sum_real, sum_imag)


def upper_level(
    top_real, top_imag, along_x, along_y, along_z, theta_map, phi_map, children, top_ids
):
    summed = None
    for octant in range(4):
        cosine, sine = octant_phase(PHASE_TOP, octant, along_x, along_y, along_z)
        cosine = cosine[:, None, :]
        sine = sine[:, None, :]
        stacked = jnp.stack(
            [top_real * cosine - top_imag * sine, top_real * sine + top_imag * cosine]
        )
        theta_done = jnp.einsum(
            "...pbt,tu->...pbu", stacked, theta_map, precision=lax.Precision.HIGHEST
        )
        phi_done = jnp.einsum(
            "...pbu,pq->...qbu", theta_done, phi_map, precision=lax.Precision.HIGHEST
        )
        select_map = (
            children[:, octant][:, None] - 4 * top_ids[:, None]
            == jnp.arange(4, dtype=jnp.int32)[None, :]
        ).astype(jnp.float32)
        placed = phi_done[..., None, :] * select_map[:, :, None]
        summed = placed if summed is None else summed + placed
    merged = summed.reshape(summed.shape[:-3] + (summed.shape[-3] * 4, summed.shape[-1]))
    return jnp.concatenate([merged[0], merged[1]], axis=-1)


def lower_level(middle, along_x, along_y, along_z, theta_map, phi_map):
    half_width = middle.shape[-1] // 2
    mid_real = middle[..., :half_width]
    mid_imag = middle[..., half_width:]
    real_parts = []
    imag_parts = []
    for octant in range(4):
        cosine, sine = octant_phase(PHASE_MID, octant, along_x, along_y, along_z)
        cosine = cosine[:, None, :]
        sine = sine[:, None, :]
        real_parts.append(mid_real * cosine - mid_imag * sine)
        imag_parts.append(mid_real * sine + mid_imag * cosine)
    stacked = jnp.stack([jnp.stack(real_parts, axis=-2), jnp.stack(imag_parts, axis=-2)])
    theta_done = jnp.einsum(
        "...pijt,tu->...piju", stacked, theta_map, precision=lax.Precision.HIGHEST
    )
    phi_done = jnp.einsum(
        "c...piju,pq->...ijqcu", theta_done, phi_map, precision=lax.Precision.HIGHEST
    )
    result_shape = phi_done.shape
    return phi_done.reshape(
        result_shape[:-5]
        + (result_shape[-5] * 4, result_shape[-3] * result_shape[-2] * result_shape[-1])
    )


def local(
    top_adj,
    level1_adj,
    image_offsets,
    image_weights,
    incidence,
    child_list,
    theta_index_top,
    theta_weight_top,
    phi_weight_top,
    theta_index_mid,
    theta_weight_mid,
    phi_weight_mid,
):
    dev_count = lax.axis_size("dev")
    dev_index = lax.axis_index("dev")
    rhs_count = lax.axis_size("rhs")
    exc_local, phi_local, top_boxes, top_width = top_adj.shape
    theta_top_count = top_width // 2
    theta_mid_count = theta_top_count // 2
    theta_low_count = theta_top_count // 4
    phi_top_count = phi_local * dev_count
    phi_mid_count = phi_top_count // 2
    phi_low_count = phi_top_count // 4
    image_total = image_offsets.shape[0] * rhs_count
    own_phi = dev_index * phi_local + jnp.arange(phi_local, dtype=jnp.int32)
    own_x, own_y, top_z = directions(theta_top_count, own_phi, phi_top_count)
    scaled = image_weights * float(image_total) ** (-0.5)
    part_real, part_imag = lattice_sum(
        image_offsets.astype(jnp.float32), scaled, incidence, own_x, own_y
    )
    sum_real, sum_imag = (
        lax.psum_scatter(part_real, "rhs", scatter_dimension=0, tiled=True),
        lax.psum_scatter(part_imag, "rhs", scatter_dimension=0, tiled=True),
    )
    sum_real = sum_real[:, :, None, :]
    sum_imag = sum_imag[:, :, None, :]
    top_real = top_adj[..., :theta_top_count]
    top_imag = top_adj[..., theta_top_count:]
    shifted = jnp.concatenate(
        [sum_real * top_real + sum_imag * top_imag, sum_real * top_imag - sum_imag * top_real],
        axis=-1,
    )
    theta_top = theta_matrix(theta_index_top, theta_weight_top, theta_mid_count)
    mid_all = jnp.arange(phi_mid_count, dtype=jnp.int32)
    mid_x, mid_y, mid_z = directions(theta_mid_count, mid_all, phi_mid_count)
    theta_mid = theta_matrix(theta_index_mid, theta_weight_mid, theta_low_count)
    phi_mid = phi_matrix(
        phi_weight_mid, mid_all, phi_low_count, jnp.arange(phi_low_count, dtype=jnp.int32)
    )
    padded = padded_2(shifted, (("dev", 1),), 2)
    padded_phi = (
        dev_index * phi_local - 2 + jnp.arange(phi_local + 4, dtype=jnp.int32)
    ) % phi_top_count
    pad_dirs = directions(theta_top_count, padded_phi, phi_top_count)
    picker = (padded_phi[:, None] == jnp.arange(phi_top_count, dtype=jnp.int32)[None, :]).astype(
        jnp.float32
    )
    pad_weight = jnp.dot(
        picker, phi_weight_top, precision=lax.Precision.HIGHEST, preferred_element_type=jnp.float32
    )
    own_mid = dev_index * (phi_local // 2) + jnp.arange(phi_local // 2, dtype=jnp.int32)
    phi_top = phi_matrix(pad_weight, padded_phi, phi_mid_count, own_mid)
    above = upper_level(
        padded[..., :theta_top_count],
        padded[..., theta_top_count:],
        pad_dirs[0],
        pad_dirs[1],
        top_z,
        theta_top,
        phi_top,
        child_list,
        jnp.arange(top_boxes, dtype=jnp.int32),
    )
    total = level1_adj + above
    return lower_level(
        lax.all_to_all(total, "dev", split_axis=2, concat_axis=1, tiled=True),
        mid_x,
        mid_y,
        mid_z,
        theta_mid,
        phi_mid,
    )


def solution(mesh):
    placed = (
        P("rhs", "dev", None, None),
        P("rhs", "dev", None, None),
        P("rhs", None),
        P("rhs"),
        P(),
        P(),
        P(),
        P(),
        P(),
        P(),
        P(),
        P(),
    )
    return jax.shard_map(
        local, mesh=mesh, in_specs=placed, out_specs=P("rhs", "dev", None), check_vma=False
    )
```

profile of v0, /device:TPU:0, one launch (start us, length us, event | category | flops | bytes accessed | tf_op | source)
XLA Modules:
  0.0 58.5 jit_solution(9289653000353431672)
XLA Ops:
  0.0 0.0 copy-start
  0.2 0.8 %slice_bitcast_fusion.2 = (f32[16]{0:T(128)S(1)}, f32[16]{0:T(128)S(1)}) fusion(f32[16,2]{0,1:T(2,128)} %param.16), kind=kLoop, calls=%fused_computation.166 | loop fusion | bytes 256 | tf_op jit(solution)/shard_map/sub | solution.py:60
  0.9 0.7 %convert_element_type.96 = f32[32,2]{0,1:T(2,128)S(1)} convert(s32[32,2]{0,1:T(2,128)} %param.14) | non-fusion elementwise | flops 64 | bytes 512 | tf_op jit(solution)/shard_map/convert_element_type | solution.py:150
  1.6 0.7 %broadcast_multiply_fusion.2 = f32[32]{0:T(128)S(1)} fusion(f32[32]{0:T(128)} %param.15), kind=kLoop, calls=%fused_computation.180 | loop fusion | flops 32 | bytes 256 | tf_op jit(solution)/shard_map/mul | solution.py:148
  2.3 0.1 broadcast_multiply_fusion.1
  2.3 0.1 broadcast_subtract_fusion
  2.4 2.3 %multiply_reduce_fusion.1 = (f32[16,2,128]{2,0,1:T(8,128)S(1)}, f32[16,2,128]{2,0,1:T(8,128)S(1)}) fusion(f32[16,2,128]{2,0,1:T(8,128)S(1)} %get-tuple-element.71, f32[32]{0:T(128)S(1)} %get-tuple-element.62, f32[16,2,128]{2,0,1:T(8,128)S(1)} %get-tuple-element.72, f32[32]{0:T(128)S(1)} %get-tuple-element.61, f32[32]{0:T(128)S(1)} %broadcast_multiply_fusion.2), kind=kLoop, calls=%fused_computation.36 | loop fusion | flops 1040384 | bytes 65920 | tf_op jit(solution)/shard_map/reduce_sum | solution.py:63
  4.8 9.9 %all-reduce.2 = (f32[16,2,128]{2,1,0:T(2,128)S(1)}, f32[16,2,128]{2,1,0:T(2,128)S(1)}) all-reduce(f32[16,2,128]{2,1,0:T(2,128)S(1)} %copy.63, f32[16,2,128]{2,1,0:T(2,128)S(1)} %copy.62), channel_id=3, replica_groups=mesh['dev'=16,'rhs'=2] {'rhs'}, use_global_device_ids=true, to_apply=%region_5.0.clone | all-reduce | flops 8192 | bytes 65536
  14.8 1.2 %dynamic-slice = u32[1]{0:T(128)} dynamic-slice(u32[32]{0:T(128)} %constant.115, u32[]{:T(128)S(6)} %add.397), dynamic_slice_sizes={1} | dynamic-slice | bytes 12
  16.7 1.0 %multiply_add_fusion.1 = (f32[8,2,16,128]{3,2,1,0:T(8,128)S(1)}, f32[8,2,16,128]{3,2,1,0:T(8,128)S(1)}) fusion(f32[8,2,16,256]{3,2,1,0:T(8,128)} %param.12, f32[8,2,128]{2,1,0:T(2,128)S(1)} %constant_dynamic-slice_fusion, f32[8,2,128]{2,1,0:T(2,128)S(1)} %constant_dynamic-slice_fusion.1), kind=kLoop, calls=%fused_computation.58 | loop fusion | flops 196608 | bytes 540672 | tf_op jit(solution)/shard_map/add | solution.py:161
  17.7 0.1 collective-permute-start
  17.8 4.4 %collective-permute-start.1 = (f32[8,2,16,256]{3,2,1,0:T(8,128)S(1)}, f32[8,2,16,256]{3,2,1,0:T(8,128)S(1)}, u32[]{:S(2)}, u32[]{:S(2)}) collective-permute-start(f32[8,2,16,256]{3,2,1,0:T(8,128)S(1)} %pad_maximum_fusion.1), channel_id=1, source_target_pairs={{2,0},{4,2},{6,4},{8,6},{10,8},{12,10},{14,12},{16,14},{18,16},{20... | collective-permute-start | bytes 786440 | tf_op jit(solution)/shard_map/ppermute | solution.py:21
  22.2 0.1 fusion.90
  22.3 0.8 %subtract_bitcast_fusion.11 = (s32[16]{0:T(128)S(1)}, s32[16]{0:T(128)S(1)}, s32[16]{0:T(128)S(1)}, s32[16]{0:T(128)S(1)}) fusion(s32[16,4]{0,1:T(4,128)} %param.17), kind=kLoop, calls=%fused_computation.161 | loop fusion | flops 80 | bytes 512 | tf_op jit(solution)/shard_map/eq | solution.py:86
  23.2 0.7 %select_reduce_fusion = f32[128,64]{0,1:T(8,128)S(1)} fusion(f32[128,3]{0,1:T(4,128)} %param.19, s32[128,3]{0,1:T(4,128)} %param.18), kind=kLoop, calls=%fused_computation.59 | loop fusion | flops 65536 | bytes 35840 | tf_op jit(solution)/shard_map/reduce_sum | solution.py:42
  23.9 0.1 fusion.51
  24.0 0.1 fusion.53
  24.1 0.0 copy-done
  24.1 0.2 fusion.4
  24.3 0.1 fusion.59
  24.5 1.9 %collective-permute-done = f32[8,2,16,256]{3,2,1,0:T(8,128)S(1)} collective-permute-done((f32[8,2,16,256]{3,2,1,0:T(8,128)S(1)}, f32[8,2,16,256]{3,2,1,0:T(8,128)S(1)}, u32[]{:S(2)}, u32[]{:S(2)}) %collective-permute-start) | collective-permute-done | bytes 262176 | tf_op jit(solution)/shard_map/ppermute | solution.py:19
  26.4 0.0 collective-permute-done.1
  26.4 0.1 pad_maximum_fusion
  26.4 0.3 subtract_bitcast_fusion.3
  26.8 0.8 %fusion.13 = f32[2,8,6,16,64]{4,3,2,1,0:T(8,128)S(1)} fusion(f32[1,8,6,16,128]{4,3,2,1,0:T(8,128)S(1)} %get-tuple-element.10, f32[1,8,6,16,128]{4,3,2,1,0:T(8,128)S(1)} %get-tuple-element.9, f32[128,64]{0,1:T(8,128)S(1)} %select_reduce_fusion), kind=kOutput, calls=%fused_computation.18 | convolution fusion | flops 151191552 | bytes 1212416 | tf_op jit(solution)/shard_map/...pbt,tu->...pbu/dot_general | solution.py:79
  27.6 1.1 %fusion.11 = f32[1,2,8,16,64]{4,0,3,2,1:T(1,128)S(1)} fusion(f32[2,8,6,16,64]{4,3,2,1,0:T(8,128)S(1)} %fusion.13, f32[6]{0:T(128)S(1)} %fusion.4), kind=kOutput, calls=%fused_computation.15 | convolution fusion | flops 1179648 | bytes 458776 | tf_op jit(solution)/shard_map/...pbu,pq->...qbu/dot_general | solution.py:82
  28.7 0.8 %fusion.17 = f32[2,8,6,16,64]{4,3,2,1,0:T(8,128)S(1)} fusion(f32[1,8,6,16,128]{4,3,2,1,0:T(8,128)S(1)} %get-tuple-element.17, f32[1,8,6,16,128]{4,3,2,1,0:T(8,128)S(1)} %get-tuple-element.18, f32[128,64]{0,1:T(8,128)S(1)} %select_reduce_fusion), kind=kOutput, calls=%fused_computation.22 | convolution fusion | flops 151191552 | bytes 1212416 | tf_op jit(solution)/shard_map/...pbt,tu->...pbu/dot_general | solution.py:79
  29.5 1.1 %fusion.9 = f32[1,2,8,16,64]{4,0,3,2,1:T(1,128)S(1)} fusion(f32[2,8,6,16,64]{4,3,2,1,0:T(8,128)S(1)} %fusion.17, f32[6]{0:T(128)S(1)} %fusion.4), kind=kOutput, calls=%fused_computation.13 | convolution fusion | flops 1179648 | bytes 458776 | tf_op jit(solution)/shard_map/...pbu,pq->...qbu/dot_general | solution.py:82
  30.6 0.8 %fusion.21 = f32[2,8,6,16,64]{4,3,2,1,0:T(8,128)S(1)} fusion(f32[1,8,6,16,128]{4,3,2,1,0:T(8,128)S(1)} %get-tuple-element.19, f32[1,8,6,16,128]{4,3,2,1,0:T(8,128)S(1)} %get-tuple-element.20, f32[128,64]{0,1:T(8,128)S(1)} %select_reduce_fusion), kind=kOutput, calls=%fused_computation.26 | convolution fusion | flops 151191552 | bytes 1212416 | tf_op jit(solution)/shard_map/...pbt,tu->...pbu/dot_general | solution.py:79
  31.4 1.1 %fusion.7 = f32[1,2,8,16,64]{4,0,3,2,1:T(1,128)S(1)} fusion(f32[2,8,6,16,64]{4,3,2,1,0:T(8,128)S(1)} %fusion.21, f32[6]{0:T(128)S(1)} %fusion.4), kind=kOutput, calls=%fused_computation.11 | convolution fusion | flops 1179648 | bytes 458776 | tf_op jit(solution)/shard_map/...pbu,pq->...qbu/dot_general | solution.py:82
  32.6 0.1 subtract_bitcast_fusion
  32.7 0.8 %fusion.25 = f32[2,8,6,16,64]{4,3,2,1,0:T(8,128)S(1)} fusion(f32[1,8,6,16,128]{4,3,2,1,0:T(8,128)S(1)} %get-tuple-element.16, f32[1,8,6,16,128]{4,3,2,1,0:T(8,128)S(1)} %get-tuple-element.15, f32[128,64]{0,1:T(8,128)S(1)} %select_reduce_fusion), kind=kOutput, calls=%fused_computation.30 | convolution fusion | flops 151191552 | bytes 1212416 | tf_op jit(solution)/shard_map/...pbt,tu->...pbu/dot_general | solution.py:79
  33.4 0.0 copy-start.1
  33.5 1.1 %fusion.5 = f32[1,2,8,16,64]{4,0,3,2,1:T(1,128)S(1)} fusion(f32[2,8,6,16,64]{4,3,2,1,0:T(8,128)S(1)} %fusion.25, f32[6]{0:T(128)S(1)} %fusion.4), kind=kOutput, calls=%fused_computation.9 | convolution fusion | flops 1179648 | bytes 458776 | tf_op jit(solution)/shard_map/...pbu,pq->...qbu/dot_general | solution.py:82
  34.6 0.0 copy-start.4
  34.6 0.0 copy-start.2
  34.6 0.0 copy-start.3
  34.6 0.4 multiply_add_fusion
  35.1 0.1 pad_maximum_fusion.2
  35.2 0.0 copy-done.1
  35.3 1.0 %copy_add_fusion = f32[8,1,64,128]{3,0,1,2:T(8,128)} fusion(f32[8,1,64,128]{3,2,1,0:T(8,128)S(1)} %pad_maximum_fusion.2, f32[8,1,64,128]{3,2,1,0:T(8,128)S(1)} %copy-done.1), kind=kLoop, calls=%fused_computation.48 | loop fusion | flops 65536 | bytes 786432 | tf_op jit(solution)/shard_map/add | solution.py:195
  36.2 5.7 %all-to-all-start = ((f32[8,1,64,128]{3,0,1,2:T(8,128)}), f32[8,1,64,128]{3,0,1,2:T(8,128)S(1)}, u32[]{:S(2)}, u32[]{:S(2)}) async-start(f32[8,1,64,128]{3,0,1,2:T(8,128)} %copy_add_fusion), calls=%async_computation | async-start | bytes 524288 | tf_op jit(solution)/shard_map/all_to_all | solution.py:197
  42.0 0.0 copy-done.4
  42.1 0.0 copy-done.2
  42.1 0.0 copy-done.3
  42.1 0.2 fusion.38
  42.3 9.7 %all-to-all-done = f32[8,1,64,128]{3,0,1,2:T(8,128)S(1)} async-done(((f32[8,1,64,128]{3,0,1,2:T(8,128)}), f32[8,1,64,128]{3,0,1,2:T(8,128)S(1)}, u32[]{:S(2)}, u32[]{:S(2)}) %all-to-all-start) | async-done | bytes 262176 | tf_op jit(solution)/shard_map/all_to_all | solution.py:197
  52.0 0.1 fusion.98
  52.1 0.4 subtract_bitcast_fusion.7
  52.5 0.1 maximum_bitcast_fusion.1
  52.7 1.8 %fusion = f32[2,8,16,4,4,32]{5,2,4,3,1,0:T(8,128)S(1)} fusion(f32[1,8,16,4,4,64]{5,2,4,3,1,0:T(8,128)S(1)} %maximum_bitcast_fusion.1, f32[64,32]{0,1:T(8,128)S(1)} %select_reduce_fusion.1, f32[8,16,4,1,64]{4,1,2,0,3:T(8,128)S(1)} %get-tuple-element.34, f32[8,16,4,1,64]{4,1,2,0,3:T(8,128)S(1)} %get-tuple-element.32, ...), kind=kOutput, calls=%fused_computation | convolution fusion | flops 101318656 | bytes 1581056 | tf_op jit(solution)/shard_map/...pijt,tu->...piju/dot_general | solution.py:108
  54.4 1.1 %convolution_bitcast_fusion = f32[8,4,4,8,2,32]{5,3,2,1,0,4:T(8,128)S(1)} fusion(f32[2,8,16,4,4,32]{5,2,4,3,1,0:T(8,128)S(1)} %fusion, f32[16,8]{0,1:T(8,128)S(1)} %select_reduce_fusion.2), kind=kOutput, calls=%fused_computation.4 | convolution fusion | flops 12582912 | bytes 786944 | tf_op jit(solution)/shard_map/c...piju,pq->...ijqcu/dot_general | solution.py:111
  55.6 0.8 %copy.72 = f32[8,4,4,8,2,32]{5,4,3,2,1,0:T(2,128)S(1)} copy(f32[8,4,4,8,2,32]{5,3,2,1,0,4:T(8,128)S(1)} %convolution_bitcast_fusion) | data formatting | bytes 524288 | tf_op jit(solution)/shard_map/c...piju,pq->...ijqcu/transpose | solution.py:111
  56.4 2.1 %reshape.1499 = f32[8,16,512]{2,1,0:T(8,128)} reshape(f32[8,4,4,8,2,32]{5,4,3,2,1,0:T(2,128)S(1)} %copy.72) | data formatting | bytes 524288 | tf_op jit(solution)/shard_map/reshape | solution.py:115
  (18 shorter events, 0.4 us)
Async XLA Ops:
  0.0 24.1 %copy-start = (f32[32,3]{0,1:T(4,128)S(1)}, f32[32,3]{0,1:T(4,128)}, u32[]{:S(2)}) copy-start(f32[32,3]{0,1:T(4,128)} %param.20) | copy-start | bytes 1156
  17.7 8.6 %collective-permute-start = (f32[8,2,16,256]{3,2,1,0:T(8,128)S(1)}, f32[8,2,16,256]{3,2,1,0:T(8,128)S(1)}, u32[]{:S(2)}, u32[]{:S(2)}) collective-permute-start(f32[8,2,16,256]{3,2,1,0:T(8,128)S(1)} %pad_maximum_fusion.1), channel_id=1, source_target_pairs={{0,2},{2,4},{4,6},{6,8},{8,10},{10,12},{12,14},{14,16},{16,18},{18... | collective-permute-start | bytes 786440 | tf_op jit(solution)/shard_map/ppermute | solution.py:19
  17.8 8.6 %collective-permute-start.1 = (f32[8,2,16,256]{3,2,1,0:T(8,128)S(1)}, f32[8,2,16,256]{3,2,1,0:T(8,128)S(1)}, u32[]{:S(2)}, u32[]{:S(2)}) collective-permute-start(f32[8,2,16,256]{3,2,1,0:T(8,128)S(1)} %pad_maximum_fusion.1), channel_id=1, source_target_pairs={{2,0},{4,2},{6,4},{8,6},{10,8},{12,10},{14,12},{16,14},{18,16},{20... | collective-permute-start | bytes 786440 | tf_op jit(solution)/shard_map/ppermute | solution.py:21
  33.4 1.8 %copy-start.1 = (f32[8,1,64,128]{3,2,1,0:T(8,128)S(1)}, f32[8,1,64,128]{3,2,1,0:T(8,128)}, u32[]{:S(2)}) copy-start(f32[8,1,64,128]{3,2,1,0:T(8,128)} %param.13) | copy-start | bytes 786436
  34.6 7.4 %copy-start.4 = (f32[16,3]{0,1:T(4,128)S(1)}, f32[16,3]{0,1:T(4,128)}, u32[]{:S(2)}) copy-start(f32[16,3]{0,1:T(4,128)} %param.23) | copy-start | bytes 580
  34.6 7.4 %copy-start.2 = (f32[64,3]{0,1:T(4,128)S(1)}, f32[64,3]{0,1:T(4,128)}, u32[]{:S(2)}) copy-start(f32[64,3]{0,1:T(4,128)} %param.22) | copy-start | bytes 2308
  34.6 7.4 %copy-start.3 = (s32[64,3]{0,1:T(4,128)S(1)}, s32[64,3]{0,1:T(4,128)}, u32[]{:S(2)}) copy-start(s32[64,3]{0,1:T(4,128)} %param.21) | copy-start | bytes 2308
  36.2 15.7 %all-to-all-start = ((f32[8,1,64,128]{3,0,1,2:T(8,128)}), f32[8,1,64,128]{3,0,1,2:T(8,128)S(1)}, u32[]{:S(2)}, u32[]{:S(2)}) async-start(f32[8,1,64,128]{3,0,1,2:T(8,128)} %copy_add_fusion), calls=%async_computation | async-start | bytes 524288 | tf_op jit(solution)/shard_map/all_to_all | solution.py:197
where the time goes:
time: 58.9 us; the launch traced here: 58.5 us
  waiting for transfers between devices  11.6 us (20%)
  matrix products  10.7 us (18%)
  starting transfers between devices  10.2 us (17%)
  blocking collectives  9.94 us (17%)
  other arithmetic  9.84 us (17%)
  local copies, waits for them, and re-layouts  5.15 us (9%)
  between operations  1.03 us (2%)
    unnamed x1, blocking collectives  9.94 us
    all_to_all x1, waiting for transfers between devices, local(): lax.all_to_all(total, 'dev', split_axis=2, concat_axis=1, tiled=True)  9.69 us
    all_to_all x1, starting transfers between devices, local(): lax.all_to_all(total, 'dev', split_axis=2, concat_axis=1, tiled=True)  5.73 us
    dot_general x4, matrix products, upper_level(): jnp.einsum('...pbu,pq->...qbu', theta_done, phi_map, precision=lax.Precis...  4.54 us
    ppermute x1, starting transfers between devices, padded_2(): lax.ppermute(head, axis, [((i + 1) % count, i) for i in range(count)])  4.43 us
    dot_general x4, matrix products, upper_level(): jnp.einsum('...pbt,tu->...pbu', stacked, theta_map, precision=lax.Precisi...  3.09 us
    reduce_sum x1, other arithmetic, lattice_sum(): jnp.sum(weighted[:, None, None, None] * jnp.cos(phase_arg), axis=0)  2.35 us
    reshape x1, local copies, waits for them, and re-layouts, lower_level(): phi_done.reshape(result_shape[:-5] + (result_shape[-5] * 4, result_shape[...  2.08 us
  transfers between devices with their start and end apart: 3, of which 2 were waited for; matrix products, arithmetic and copies ran while one was open for 4% of the time, Pallas kernels for 0%

commit v1 on v0

--- a/solution.py
+++ b/solution.py
@@ -3,6 +3,7 @@
 import jax.numpy as jnp
 from jax import lax
 from jax.sharding import PartitionSpec as P
+from jax.lax import all_to_all, axis_size
 
 PHASE_TOP = 18.85
 PHASE_MID = 9.42
@@ -194,7 +195,15 @@
     )
     total = level1_adj + above
     return lower_level(
-        lax.all_to_all(total, "dev", split_axis=2, concat_axis=1, tiled=True),
+        jnp.concatenate(
+            all_to_all(
+                jnp.stack(jnp.split(total, axis_size("dev"), axis=2), 0),
+                split_axis=0,
+                concat_axis=0,
+                axis_name="dev",
+            ),
+            1,
+        ),
         mid_x,
         mid_y,
         mid_z,

time: 58.9 us -> 67.8 us (1.15)
  local copies, waits for them, and re-layouts: 5.15 us -> 14.9 us
  other arithmetic: 9.84 us -> 8.93 us
    unnamed x13 -> x28, local copies, waits for them, and re-layouts: 1.29 us -> 10.4 us
    add x1, other arithmetic: 1 us -> 0.14 us  [local(): total = level1_adj + above]
where the time goes in v1:
time: 67.8 us; the launch traced here: 67.4 us
  local copies, waits for them, and re-layouts  14.9 us (22%)
  waiting for transfers between devices  11.6 us (17%)
  matrix products  10.7 us (16%)
  starting transfers between devices  10.2 us (15%)
  blocking collectives  9.94 us (15%)
  other arithmetic  8.93 us (13%)
  between operations  1.04 us (2%)
    unnamed x28, local copies, waits for them, and re-layouts  10.4 us
    unnamed x1, blocking collectives  9.94 us
    all_to_all x1, waiting for transfers between devices, local(): all_to_all(jnp.stack(jnp.split(total, axis_size('dev'), axis=2), 0), spli...  9.69 us
    all_to_all x1, starting transfers between devices, local(): all_to_all(jnp.stack(jnp.split(total, axis_size('dev'), axis=2), 0), spli...  5.73 us
    dot_general x4, matrix products, upper_level(): jnp.einsum('...pbu,pq->...qbu', theta_done, phi_map, precision=lax.Precis...  4.54 us
    ppermute x1, starting transfers between devices, padded_2(): lax.ppermute(head, axis, [((i + 1) % count, i) for i in range(count)])  4.43 us
    dot_general x4, matrix products, upper_level(): jnp.einsum('...pbt,tu->...pbu', stacked, theta_map, precision=lax.Precisi...  3.08 us
    reduce_sum x1, other arithmetic, lattice_sum(): jnp.sum(weighted[:, None, None, None] * jnp.cos(phase_arg), axis=0)  2.35 us
  transfers between devices with their start and end apart: 3, of which 2 were waited for; matrix products, arithmetic and copies ran while one was open for 4% of the time, Pallas kernels for 0%

profile of v1, /device:TPU:0, one launch (start us, length us, event | category | flops | bytes accessed | tf_op | source)
XLA Modules:
  0.0 67.4 jit_solution(13956764866630584606)
XLA Ops:
  0.2 0.8 %slice_bitcast_fusion.18 = (f32[16]{0:T(128)S(1)}, f32[16]{0:T(128)S(1)}) fusion(f32[16,2]{0,1:T(2,128)} %param.16), kind=kLoop, calls=%fused_computation.198 | loop fusion | bytes 256 | tf_op jit(solution)/shard_map/sub | solution.py:61
  0.9 0.7 %convert_element_type.96 = f32[32,2]{0,1:T(2,128)S(1)} convert(s32[32,2]{0,1:T(2,128)} %param.14) | non-fusion elementwise | flops 64 | bytes 512 | tf_op jit(solution)/shard_map/convert_element_type | solution.py:151
  1.6 0.7 broadcast_multiply_fusion.2
  2.3 0.1 broadcast_multiply_fusion.1
  2.3 0.1 broadcast_subtract_fusion
  2.4 2.3 %multiply_reduce_fusion.1 = (f32[16,2,128]{2,0,1:T(8,128)S(1)}, f32[16,2,128]{2,0,1:T(8,128)S(1)}) fusion(f32[16,2,128]{2,0,1:T(8,128)S(1)} %get-tuple-element.67, f32[32]{0:T(128)S(1)} %get-tuple-element.58, f32[16,2,128]{2,0,1:T(8,128)S(1)} %get-tuple-element.68, f32[32]{0:T(128)S(1)} %get-tuple-element.57, f32[32]{0:T(128)S(1)} %broadcast_multiply_fusion.2), kind=kLoop, calls=%fused_computation.36 | loop fusion | flops 1040384 | bytes 65920 | tf_op jit(solution)/shard_map/reduce_sum | solution.py:64
  4.8 9.9 %all-reduce.2 = (f32[16,2,128]{2,1,0:T(2,128)S(1)}, f32[16,2,128]{2,1,0:T(2,128)S(1)}) all-reduce(f32[16,2,128]{2,1,0:T(2,128)S(1)} %copy.93, f32[16,2,128]{2,1,0:T(2,128)S(1)} %copy.92), channel_id=3, replica_groups=mesh['dev'=16,'rhs'=2] {'rhs'}, use_global_device_ids=true, to_apply=%region_5.0.clone | all-reduce | flops 8192 | bytes 65536
  14.8 1.2 %dynamic-slice = u32[1]{0:T(128)} dynamic-slice(u32[32]{0:T(128)} %constant.115, u32[]{:T(128)S(6)} %add.397), dynamic_slice_sizes={1} | dynamic-slice | bytes 12
  16.7 1.0 %multiply_add_fusion.1 = (f32[8,2,16,128]{3,2,1,0:T(8,128)S(1)}, f32[8,2,16,128]{3,2,1,0:T(8,128)S(1)}) fusion(f32[8,2,16,256]{3,2,1,0:T(8,128)} %param.12, f32[8,2,128]{2,1,0:T(2,128)S(1)} %constant_dynamic-slice_fusion, f32[8,2,128]{2,1,0:T(2,128)S(1)} %constant_dynamic-slice_fusion.1), kind=kLoop, calls=%fused_computation.58 | loop fusion | flops 196608 | bytes 540672 | tf_op jit(solution)/shard_map/add | solution.py:162
  17.7 0.1 collective-permute-start
  17.8 4.4 %collective-permute-start.1 = (f32[8,2,16,256]{3,2,1,0:T(8,128)S(1)}, f32[8,2,16,256]{3,2,1,0:T(8,128)S(1)}, u32[]{:S(2)}, u32[]{:S(2)}) collective-permute-start(f32[8,2,16,256]{3,2,1,0:T(8,128)S(1)} %pad_maximum_fusion.1), channel_id=1, source_target_pairs={{2,0},{4,2},{6,4},{8,6},{10,8},{12,10},{14,12},{16,14},{18,16},{20... | collective-permute-start | bytes 786440 | tf_op jit(solution)/shard_map/ppermute | solution.py:22
  22.2 0.1 fusion.90
  22.3 0.8 %subtract_bitcast_fusion.11 = (s32[16]{0:T(128)S(1)}, s32[16]{0:T(128)S(1)}, s32[16]{0:T(128)S(1)}, s32[16]{0:T(128)S(1)}) fusion(s32[16,4]{0,1:T(4,128)} %param.17), kind=kLoop, calls=%fused_computation.193 | loop fusion | flops 80 | bytes 512 | tf_op jit(solution)/shard_map/eq | solution.py:87
  23.2 0.7 %select_reduce_fusion = f32[128,64]{0,1:T(8,128)S(1)} fusion(f32[128,3]{0,1:T(4,128)} %param.19, s32[128,3]{0,1:T(4,128)} %param.18), kind=kLoop, calls=%fused_computation.59 | loop fusion | flops 65536 | bytes 35840 | tf_op jit(solution)/shard_map/reduce_sum | solution.py:43
  23.9 0.1 fusion.51
  24.0 0.1 fusion.53
  24.1 0.2 fusion.4
  24.3 0.1 fusion.59
  24.5 1.9 %collective-permute-done = f32[8,2,16,256]{3,2,1,0:T(8,128)S(1)} collective-permute-done((f32[8,2,16,256]{3,2,1,0:T(8,128)S(1)}, f32[8,2,16,256]{3,2,1,0:T(8,128)S(1)}, u32[]{:S(2)}, u32[]{:S(2)}) %collective-permute-start) | collective-permute-done | bytes 262176 | tf_op jit(solution)/shard_map/ppermute | solution.py:20
  26.4 0.0 collective-permute-done.1
  26.4 0.1 pad_maximum_fusion
  26.4 0.3 subtract_bitcast_fusion.3
  26.8 0.8 %fusion.13 = f32[2,8,6,16,64]{4,3,2,1,0:T(8,128)S(1)} fusion(f32[1,8,6,16,128]{4,3,2,1,0:T(8,128)S(1)} %get-tuple-element.10, f32[1,8,6,16,128]{4,3,2,1,0:T(8,128)S(1)} %get-tuple-element.9, f32[128,64]{0,1:T(8,128)S(1)} %select_reduce_fusion), kind=kOutput, calls=%fused_computation.18 | convolution fusion | flops 151191552 | bytes 1212416 | tf_op jit(solution)/shard_map/...pbt,tu->...pbu/dot_general | solution.py:80
  27.6 1.1 %fusion.11 = f32[1,2,8,16,64]{4,0,3,2,1:T(1,128)S(1)} fusion(f32[2,8,6,16,64]{4,3,2,1,0:T(8,128)S(1)} %fusion.13, f32[6]{0:T(128)S(1)} %fusion.4), kind=kOutput, calls=%fused_computation.15 | convolution fusion | flops 1179648 | bytes 458776 | tf_op jit(solution)/shard_map/...pbu,pq->...qbu/dot_general | solution.py:83
  28.7 0.8 %fusion.17 = f32[2,8,6,16,64]{4,3,2,1,0:T(8,128)S(1)} fusion(f32[1,8,6,16,128]{4,3,2,1,0:T(8,128)S(1)} %get-tuple-element.17, f32[1,8,6,16,128]{4,3,2,1,0:T(8,128)S(1)} %get-tuple-element.18, f32[128,64]{0,1:T(8,128)S(1)} %select_reduce_fusion), kind=kOutput, calls=%fused_computation.22 | convolution fusion | flops 151191552 | bytes 1212416 | tf_op jit(solution)/shard_map/...pbt,tu->...pbu/dot_general | solution.py:80
  29.5 1.1 %fusion.9 = f32[1,2,8,16,64]{4,0,3,2,1:T(1,128)S(1)} fusion(f32[2,8,6,16,64]{4,3,2,1,0:T(8,128)S(1)} %fusion.17, f32[6]{0:T(128)S(1)} %fusion.4), kind=kOutput, calls=%fused_computation.13 | convolution fusion | flops 1179648 | bytes 458776 | tf_op jit(solution)/shard_map/...pbu,pq->...qbu/dot_general | solution.py:83
  30.6 0.8 %fusion.21 = f32[2,8,6,16,64]{4,3,2,1,0:T(8,128)S(1)} fusion(f32[1,8,6,16,128]{4,3,2,1,0:T(8,128)S(1)} %get-tuple-element.19, f32[1,8,6,16,128]{4,3,2,1,0:T(8,128)S(1)} %get-tuple-element.20, f32[128,64]{0,1:T(8,128)S(1)} %select_reduce_fusion), kind=kOutput, calls=%fused_computation.26 | convolution fusion | flops 151191552 | bytes 1212416 | tf_op jit(solution)/shard_map/...pbt,tu->...pbu/dot_general | solution.py:80
  31.4 1.1 %fusion.7 = f32[1,2,8,16,64]{4,0,3,2,1:T(1,128)S(1)} fusion(f32[2,8,6,16,64]{4,3,2,1,0:T(8,128)S(1)} %fusion.21, f32[6]{0:T(128)S(1)} %fusion.4), kind=kOutput, calls=%fused_computation.11 | convolution fusion | flops 1179648 | bytes 458776 | tf_op jit(solution)/shard_map/...pbu,pq->...qbu/dot_general | solution.py:83
  32.6 0.1 subtract_bitcast_fusion
  32.7 0.0 copy-start.1
  32.7 0.8 %fusion.25 = f32[2,8,6,16,64]{4,3,2,1,0:T(8,128)S(1)} fusion(f32[1,8,6,16,128]{4,3,2,1,0:T(8,128)S(1)} %get-tuple-element.16, f32[1,8,6,16,128]{4,3,2,1,0:T(8,128)S(1)} %get-tuple-element.15, f32[128,64]{0,1:T(8,128)S(1)} %select_reduce_fusion), kind=kOutput, calls=%fused_computation.30 | convolution fusion | flops 151191552 | bytes 1212416 | tf_op jit(solution)/shard_map/...pbt,tu->...pbu/dot_general | solution.py:80
  33.5 1.1 %fusion.5 = f32[1,2,8,16,64]{4,0,3,2,1:T(1,128)S(1)} fusion(f32[2,8,6,16,64]{4,3,2,1,0:T(8,128)S(1)} %fusion.25, f32[6]{0:T(128)S(1)} %fusion.4), kind=kOutput, calls=%fused_computation.9 | convolution fusion | flops 1179648 | bytes 458776 | tf_op jit(solution)/shard_map/...pbu,pq->...qbu/dot_general | solution.py:83
  34.6 0.0 copy-start.4
  34.6 0.0 copy-start.2
  34.6 0.0 copy-start.3
  34.6 0.4 multiply_add_fusion
  35.1 0.1 maximum_add_fusion
  35.2 0.6 constant_dynamic-update-slice_fusion.15
  35.9 0.6 constant_dynamic-update-slice_fusion.14
  36.5 0.6 constant_dynamic-update-slice_fusion.13
  37.1 0.6 constant_dynamic-update-slice_fusion.12
  37.7 0.6 constant_dynamic-update-slice_fusion.11
  38.3 0.6 constant_dynamic-update-slice_fusion.10
  38.9 0.6 constant_dynamic-update-slice_fusion.9
  39.5 0.6 constant_dynamic-update-slice_fusion.8
  40.1 0.6 constant_dynamic-update-slice_fusion.7
  40.7 0.6 constant_dynamic-update-slice_fusion.6
  41.4 0.6 constant_dynamic-update-slice_fusion.5
  42.0 0.6 constant_dynamic-update-slice_fusion.4
  42.6 0.6 constant_dynamic-update-slice_fusion.3
  43.2 0.6 constant_dynamic-update-slice_fusion.2
  43.8 0.6 constant_dynamic-update-slice_fusion.1
  44.4 0.6 constant_dynamic-update-slice_fusion
  45.0 5.7 %all-to-all-start = ((f32[16,8,1,4,128]{4,3,1,2,0:T(4,128)}), f32[16,8,1,4,128]{4,3,1,2,0:T(4,128)S(1)}, u32[]{:S(2)}, u32[]{:S(2)}) async-start(f32[16,8,1,4,128]{4,3,1,2,0:T(4,128)} %constant_dynamic-update-slice_fusion), calls=%async_computation | async-start | bytes 524288 | tf_op jit(solution)/shard_map/all_to_all | solution.py:199
  50.9 0.2 fusion.38
  51.1 9.7 %all-to-all-done = f32[16,8,1,4,128]{4,3,1,2,0:T(4,128)S(1)} async-done(((f32[16,8,1,4,128]{4,3,1,2,0:T(4,128)}), f32[16,8,1,4,128]{4,3,1,2,0:T(4,128)S(1)}, u32[]{:S(2)}, u32[]{:S(2)}) %all-to-all-start) | async-done | bytes 262176 | tf_op jit(solution)/shard_map/all_to_all | solution.py:199
  60.8 0.2 copy.128
  60.9 0.1 subtract_bitcast_fusion.6
  61.1 0.4 subtract_bitcast_fusion.7
  61.4 0.1 maximum_bitcast_fusion.1
  61.6 1.8 %fusion = f32[2,8,16,4,4,32]{5,2,4,3,1,0:T(8,128)S(1)} fusion(f32[1,8,16,4,4,64]{5,2,4,3,1,0:T(8,128)S(1)} %maximum_bitcast_fusion.1, f32[64,32]{0,1:T(8,128)S(1)} %select_reduce_fusion.1, f32[8,16,4,1,64]{4,1,2,0,3:T(8,128)S(1)} %get-tuple-element.36, f32[8,16,4,1,64]{4,1,2,0,3:T(8,128)S(1)} %get-tuple-element.34, ...), kind=kOutput, calls=%fused_computation | convolution fusion | flops 101318656 | bytes 1581056 | tf_op jit(solution)/shard_map/...pijt,tu->...piju/dot_general | solution.py:109
  63.3 1.1 %convolution_bitcast_fusion = f32[8,4,4,8,2,32]{5,3,2,1,0,4:T(8,128)S(1)} fusion(f32[2,8,16,4,4,32]{5,2,4,3,1,0:T(8,128)S(1)} %fusion, f32[16,8]{0,1:T(8,128)S(1)} %select_reduce_fusion.2), kind=kOutput, calls=%fused_computation.4 | convolution fusion | flops 12582912 | bytes 786944 | tf_op jit(solution)/shard_map/c...piju,pq->...ijqcu/dot_general | solution.py:112
  64.5 0.8 %copy.100 = f32[8,4,4,8,2,32]{5,4,3,2,1,0:T(2,128)S(1)} copy(f32[8,4,4,8,2,32]{5,3,2,1,0,4:T(8,128)S(1)} %convolution_bitcast_fusion) | data formatting | bytes 524288 | tf_op jit(solution)/shard_map/c...piju,pq->...ijqcu/transpose | solution.py:112
  65.3 2.1 %reshape.1504 = f32[8,16,512]{2,1,0:T(8,128)} reshape(f32[8,4,4,8,2,32]{5,4,3,2,1,0:T(2,128)S(1)} %copy.100) | data formatting | bytes 524288 | tf_op jit(solution)/shard_map/reshape | solution.py:116
  (24 shorter events, 0.4 us)
Async XLA Ops:
  0.0 24.1 %copy-start = (f32[32,3]{0,1:T(4,128)S(1)}, f32[32,3]{0,1:T(4,128)}, u32[]{:S(2)}) copy-start(f32[32,3]{0,1:T(4,128)} %param.20) | copy-start | bytes 1156
  17.7 8.6 %collective-permute-start = (f32[8,2,16,256]{3,2,1,0:T(8,128)S(1)}, f32[8,2,16,256]{3,2,1,0:T(8,128)S(1)}, u32[]{:S(2)}, u32[]{:S(2)}) collective-permute-start(f32[8,2,16,256]{3,2,1,0:T(8,128)S(1)} %pad_maximum_fusion.1), channel_id=1, source_target_pairs={{0,2},{2,4},{4,6},{6,8},{8,10},{10,12},{12,14},{14,16},{16,18},{18... | collective-permute-start | bytes 786440 | tf_op jit(solution)/shard_map/ppermute | solution.py:20
  17.8 8.6 %collective-permute-start.1 = (f32[8,2,16,256]{3,2,1,0:T(8,128)S(1)}, f32[8,2,16,256]{3,2,1,0:T(8,128)S(1)}, u32[]{:S(2)}, u32[]{:S(2)}) collective-permute-start(f32[8,2,16,256]{3,2,1,0:T(8,128)S(1)} %pad_maximum_fusion.1), channel_id=1, source_target_pairs={{2,0},{4,2},{6,4},{8,6},{10,8},{12,10},{14,12},{16,14},{18,16},{20... | collective-permute-start | bytes 786440 | tf_op jit(solution)/shard_map/ppermute | solution.py:22
  32.7 2.4 %copy-start.1 = (f32[8,1,64,128]{3,2,1,0:T(8,128)S(1)}, f32[8,1,64,128]{3,2,1,0:T(8,128)}, u32[]{:S(2)}) copy-start(f32[8,1,64,128]{3,2,1,0:T(8,128)} %param.13) | copy-start | bytes 786436
  34.6 16.2 %copy-start.4 = (f32[16,3]{0,1:T(4,128)S(1)}, f32[16,3]{0,1:T(4,128)}, u32[]{:S(2)}) copy-start(f32[16,3]{0,1:T(4,128)} %param.23) | copy-start | bytes 580
  34.6 16.2 %copy-start.2 = (f32[64,3]{0,1:T(4,128)S(1)}, f32[64,3]{0,1:T(4,128)}, u32[]{:S(2)}) copy-start(f32[64,3]{0,1:T(4,128)} %param.22) | copy-start | bytes 2308
  34.6 16.2 %copy-start.3 = (s32[64,3]{0,1:T(4,128)S(1)}, s32[64,3]{0,1:T(4,128)}, u32[]{:S(2)}) copy-start(s32[64,3]{0,1:T(4,128)} %param.21) | copy-start | bytes 2308
  45.0 15.7 %all-to-all-start = ((f32[16,8,1,4,128]{4,3,1,2,0:T(4,128)}), f32[16,8,1,4,128]{4,3,1,2,0:T(4,128)S(1)}, u32[]{:S(2)}, u32[]{:S(2)}) async-start(f32[16,8,1,4,128]{4,3,1,2,0:T(4,128)} %constant_dynamic-update-slice_fusion), calls=%async_computation | async-start | bytes 524288 | tf_op jit(solution)/shard_map/all_to_all | solution.py:199
